TPU v7x, 32 devices: a whole 2x2x4 slice. The times are simulated.
32 devices in a mesh: groups: 2 (over y), tensor: 4 (over z), dp: 4 (over x, core).
Axes of the slice: x: 2, y: 2, z: 4, core: 2. Of those that a mesh axis runs over, the one named last changes fastest.
Arguments:
- tokens: bfloat16 [256, 8192], P(('groups', 'tensor', 'dp')), parts along dimension 0, may hold values from -6 to 6
- gate_projection_matrix: bfloat16 [8192, 14336], P('dp', 'tensor'), may hold values from -0.0625 to 0.0625
- up_projection_matrix: bfloat16 [8192, 14336], P('dp', 'tensor'), may hold values from -0.0625 to 0.0625
- down_projection_matrix: bfloat16 [14336, 8192], P('tensor', 'dp'), may hold values from -0.046875 to 0.046875
- gate_adapter_inmap: bfloat16 [16384, 64], P(('groups', 'dp')), parts along dimension 0, may hold values from -0.0625 to 0.0625
- gate_adapter_outmap: bfloat16 [64, 28672], P(None, ('groups', 'tensor')), parts along dimension 1, may hold values from -0.75 to 0.75
- up_adapter_inmap: bfloat16 [16384, 64], P(('groups', 'dp')), parts along dimension 0, may hold values from -0.0625 to 0.0625
- up_adapter_outmap: bfloat16 [64, 28672], P(None, ('groups', 'tensor')), parts along dimension 1, may hold values from -0.75 to 0.75
- down_adapter_inmap: bfloat16 [28672, 64], P(('groups', 'tensor')), parts along dimension 0, may hold values from -0.046875 to 0.046875
- down_adapter_outmap: bfloat16 [64, 16384], P(None, 'groups'), parts along dimension 1, may hold values from -0.75 to 0.75
Outputs:
- block_out: bfloat16 [256, 8192], P(('groups', 'tensor', 'dp')), parts along dimension 0
There are 2 independent parts, one for each index of `groups`. A program takes and returns all parts, laid end to end along the dimension named above; an argument that names none is the same for every part. Nothing has to cross between parts.
All inputs are finite; a program needn't handle non-finite values.
Results may differ from a plain program's by a relative error of at most 0.0053.
Values may be sent and summed in bfloat16 or wider, within the bound.
A program may use at most 256 MiB of HBM per device.

v0:
```python
import jax
import jax.numpy as jnp
from jax import lax
from jax.sharding import PartitionSpec as P

adapter_scale_factor = 0.5


def body(
    tokens,
    gate_projection_matrix,
    up_projection_matrix,
    down_projection_matrix,
    gate_adapter_inmap,
    gate_adapter_outmap,
    up_adapter_inmap,
    up_adapter_outmap,
    down_adapter_inmap,
    down_adapter_outmap,
):
    adapter_rank_size = gate_adapter_inmap.shape[1]
    columns = lax.all_to_all(tokens, "dp", split_axis=1, concat_axis=0, tiled=True)
    gathered = lax.all_gather(columns, "tensor", axis=0, tiled=True)

    def summed(weights):
        partial = jnp.dot(gathered, weights, preferred_element_type=jnp.float32)
        return lax.psum_scatter(partial, "dp", scatter_dimension=0, tiled=True)

    gate_dense_part = summed(gate_projection_matrix)
    up_dense_part = summed(up_projection_matrix)
    lowrank = summed(jnp.concatenate([gate_adapter_inmap, up_adapter_inmap], axis=1)).astype(
        jnp.bfloat16
    )
    gate_lowrank_part = lowrank[:, :adapter_rank_size]
    up_lowrank_part = lowrank[:, adapter_rank_size:]
    gate_activated = gate_dense_part + adapter_scale_factor * jnp.dot(
        gate_lowrank_part, gate_adapter_outmap, preferred_element_type=jnp.float32
    )
    up_projected_value = up_dense_part + adapter_scale_factor * jnp.dot(
        up_lowrank_part, up_adapter_outmap, preferred_element_type=jnp.float32
    )
    hidden_product = (jax.nn.silu(gate_activated) * up_projected_value).astype(jnp.bfloat16)
    hidden_all = lax.all_gather(hidden_product, "dp", axis=0, tiled=True)
    low = jnp.dot(hidden_all, down_adapter_inmap, preferred_element_type=jnp.float32)
    width = down_projection_matrix.shape[1]
    own_map = lax.dynamic_slice_in_dim(
        down_adapter_outmap, lax.axis_index("dp") * width, width, axis=1
    ).astype(jnp.float32)
    term = jnp.dot(hidden_all, down_projection_matrix, preferred_element_type=jnp.float32)
    term = term + adapter_scale_factor * jnp.dot(low, own_map, precision=lax.Precision.HIGHEST)
    rows_out = lax.psum_scatter(term, "tensor", scatter_dimension=0, tiled=True)
    return lax.all_to_all(
        rows_out.astype(jnp.bfloat16), "dp", split_axis=0, concat_axis=1, tiled=True
    )


def solution(mesh):
    placed = (
        P(("groups", "tensor", "dp"), None),
        P("dp", "tensor"),
        P("dp", "tensor"),
        P("tensor", "dp"),
        P(("groups", "dp"), None),
        P(None, ("groups", "tensor")),
        P(("groups", "dp"), None),
        P(None, ("groups", "tensor")),
        P(("groups", "tensor"), None),
        P(None, "groups"),
    )
    return jax.shard_map(
        body,
        mesh=mesh,
        in_specs=placed,
        out_specs=P(("groups", "tensor", "dp"), None),
        check_vma=False,
    )
```

profile of v0, /device:TPU:0, one launch (start us, length us, event | category | flops | bytes accessed | tf_op | source)
XLA Modules:
  0.0 181.7 jit_solution(13152078661154141634)
XLA Ops:
  6.5 0.0 copy-start
  6.5 0.0 reduce-scatter.13.cloned.1.call-start
  6.5 9.0 %all_to_all.38 = bf16[8,4,2048]{2,0,1:T(8,128)(2,1)S(1)} all-to-all(bf16[8,4,2048]{2,0,1:T(8,128)(2,1)} %bitcast.26), channel_id=1, replica_groups=mesh['groups'=2,'tensor'=4,'dp'=4] {'dp'}, dimensions={1} | all-to-all | bytes 262144 | tf_op jit(solution)/shard_map/all_to_all | solution.py:22
  15.5 16.2 %all_gather.6 = bf16[128,2048]{1,0:T(8,128)(2,1)S(1)} all-gather(bf16[32,2048]{1,0:T(8,128)(2,1)S(1)} %bitcast.24), channel_id=1, replica_groups=mesh['groups'=2,'tensor'=4,'dp'=4] {'tensor'}, dimensions={0}, use_global_device_ids=true | all-gather | bytes 655360 | tf_op jit(solution)/shard_map/all_gather | solution.py:23
  31.7 1.3 convolution_bitcast_fusion
  33.0 0.7 copy.11
  33.7 0.0 reduce-scatter.13.cloned.1.call-update
  33.8 0.0 reduce-scatter.7.cloned.1.call-start
  33.8 8.5 %fusion.13 = f32[128,3584]{1,0:T(8,128)} fusion(bf16[128,2048]{1,0:T(8,128)(2,1)S(1)} %all_gather.6, bf16[2048,3584]{1,0:T(8,128)(2,1)} %param.11), kind=kOutput, calls=%fused_computation.18 | convolution fusion | flops 1879048192 | bytes 17039360 | tf_op jit(solution)/shard_map/dot_general | solution.py:26
  42.3 0.0 copy-start.2
  42.3 0.0 copy-start.3
  42.3 0.0 reduce-scatter.7.cloned.1.call-update
  42.3 0.0 reduce-scatter.9.cloned.1.call-start
  42.4 8.6 %fusion.14 = f32[128,3584]{1,0:T(8,128)} fusion(bf16[128,2048]{1,0:T(8,128)(2,1)S(1)} %all_gather.6, bf16[2048,3584]{1,0:T(8,128)(2,1)} %param.12), kind=kOutput, calls=%fused_computation.19 | convolution fusion | flops 1879048192 | bytes 17039360 | tf_op jit(solution)/shard_map/dot_general | solution.py:26
  51.0 0.0 copy-start.1
  51.0 0.0 reduce-scatter.9.cloned.1.call-update
  51.0 0.0 reduce-scatter.11.cloned.1.call-start
  51.1 3.4 %reduce-scatter.13.cloned.1.call-done = f32[32,128]{1,0:T(8,128)} async-done(((f32[128,128]{1,0:T(8,128)}), f32[32,128]{1,0:T(8,128)}) %reduce-scatter.13.cloned.1.call-update) | async-done | bytes 16400
  54.5 0.8 copy.12
  55.3 31.4 %reduce-scatter.7.cloned.1.call-done = f32[32,3584]{1,0:T(8,128)} async-done(((f32[128,3584]{1,0:T(8,128)}), f32[32,3584]{1,0:T(8,128)}) %reduce-scatter.7.cloned.1.call-update) | async-done | bytes 458768 | tf_op jit(solution)/shard_map/reduce_scatter | solution.py:27
  86.7 0.0 copy-done.2
  86.7 1.3 fusion.2
  88.0 30.9 %reduce-scatter.9.cloned.1.call-done = f32[32,3584]{1,0:T(8,128)} async-done(((f32[128,3584]{1,0:T(8,128)}), f32[32,3584]{1,0:T(8,128)}) %reduce-scatter.9.cloned.1.call-update) | async-done | bytes 458768 | tf_op jit(solution)/shard_map/reduce_scatter | solution.py:27
  118.9 0.0 copy-done.3
  118.9 1.3 fusion.3
  120.2 8.7 %all_gather.7 = bf16[128,3584]{1,0:T(8,128)(2,1)S(1)} all-gather(bf16[32,3584]{1,0:T(8,128)(2,1)S(1)} %fusion.3), channel_id=1, replica_groups=mesh['groups'=2,'tensor'=4,'dp'=4] {'dp'}, dimensions={0}, use_global_device_ids=true | all-gather | bytes 1146880 | tf_op jit(solution)/shard_map/all_gather | solution.py:43
  128.9 7.5 %fusion.15 = f32[128,2048]{1,0:T(8,128)S(1)} fusion(bf16[128,3584]{1,0:T(8,128)(2,1)S(1)} %all_gather.7, bf16[3584,2048]{1,0:T(8,128)(2,1)} %param.13), kind=kOutput, calls=%fused_computation.20 | convolution fusion | flops 1879048192 | bytes 16646144 | tf_op jit(solution)/shard_map/dot_general | solution.py:49
  136.4 0.0 copy-done.1
  136.4 0.4 fusion.16
  136.8 0.0 copy-done
  136.8 1.6 fusion.4
  138.4 0.0 reduce-scatter.11.cloned.1.call-update
  138.4 28.0 %reduce-scatter.11.cloned.1.call-done = f32[32,2048]{1,0:T(8,128)} async-done(((f32[128,2048]{1,0:T(8,128)}), f32[32,2048]{1,0:T(8,128)}) %reduce-scatter.11.cloned.1.call-update) | async-done | bytes 262160 | tf_op jit(solution)/shard_map/reduce_scatter | solution.py:51
  166.4 1.0 convert_bitcast_fusion
  167.4 7.1 %all_to_all.39 = bf16[4,8,2048]{2,1,0:T(8,128)(2,1)S(1)} all-to-all(bf16[4,8,2048]{2,1,0:T(8,128)(2,1)S(1)} %convert_bitcast_fusion), channel_id=1, replica_groups=mesh['groups'=2,'tensor'=4,'dp'=4] {'dp'}, dimensions={0} | all-to-all | bytes 262144 | tf_op jit(solution)/shard_map/all_to_all | solution.py:52
  174.5 0.7 copy.14
Async XLA Ops:
  6.5 130.3 %copy-start = (bf16[64,8192]{1,0:T(8,128)(2,1)S(1)}, bf16[64,8192]{1,0:T(8,128)(2,1)}, u32[]{:S(2)}) copy-start(bf16[64,8192]{1,0:T(8,128)(2,1)} %param.19) | copy-start | bytes 3145732
  6.5 47.9 %reduce-scatter.13.cloned.1.call-start = ((), (), s32[]{:S(2)}) async-start(), calls=%async_computation.9 | async-start | bytes 81920
  33.8 52.9 %reduce-scatter.7.cloned.1.call-start = ((), (), s32[]{:S(2)}) async-start(), calls=%async_computation.6 | async-start | bytes 2293760 | tf_op jit(solution)/shard_map/reduce_scatter | solution.py:27
  42.3 44.4 %copy-start.2 = (bf16[64,3584]{1,0:T(8,128)(2,1)S(1)}, bf16[64,3584]{1,0:T(8,128)(2,1)}, u32[]{:S(2)}) copy-start(bf16[64,3584]{1,0:T(8,128)(2,1)} %param.15) | copy-start | bytes 1376260
  42.3 76.6 %copy-start.3 = (bf16[64,3584]{1,0:T(8,128)(2,1)S(1)}, bf16[64,3584]{1,0:T(8,128)(2,1)}, u32[]{:S(2)}) copy-start(bf16[64,3584]{1,0:T(8,128)(2,1)} %param.17) | copy-start | bytes 1376260
  42.3 76.5 %reduce-scatter.9.cloned.1.call-start = ((), (), s32[]{:S(2)}) async-start(), calls=%async_computation.7 | async-start | bytes 2293760 | tf_op jit(solution)/shard_map/reduce_scatter | solution.py:27
  51.0 85.5 %copy-start.1 = (bf16[3584,64]{0,1:T(8,128)(2,1)S(1)}, bf16[3584,64]{0,1:T(8,128)(2,1)}, u32[]{:S(2)}) copy-start(bf16[3584,64]{0,1:T(8,128)(2,1)} %param.18) | copy-start | bytes 1376260
  51.0 115.4 %reduce-scatter.11.cloned.1.call-start = ((), (), s32[]{:S(2)}) async-start(), calls=%async_computation.8 | async-start | bytes 1310720 | tf_op jit(solution)/shard_map/reduce_scatter | solution.py:51
Sparse Core Ops, SparseCore 0:
  33.9 20.5 reduce-scatter.12
  57.0 29.6 reduce-scatter.6
  89.2 29.5 reduce-scatter.8
  138.5 27.8 reduce-scatter.10
where the time goes:
time: 182 us
  waiting for transfers between devices  93.8 us (52%)
  blocking collectives  41 us (23%)
  matrix products  30.4 us (17%)
  between operations  13.2 us (7%)
  local copies, waits for them, and re-layouts  2.23 us (1%)
    reduce_scatter x2, waiting for transfers between devices, summed(): return lax.psum_scatter(partial, 'dp', scatter_dimension=0, tiled=True)  62.3 us
    reduce_scatter x1, waiting for transfers between devices, body(): rows_out = lax.psum_scatter(term, 'tensor', scatter_dimension=0, tiled=True)  28 us
    dot_general x3, matrix products, summed(): partial = jnp.dot(gathered, weights, preferred_element_type=jnp.float32)  18.4 us
    all_gather x1, blocking collectives, body(): gathered = lax.all_gather(columns, 'tensor', axis=0, tiled=True)  16.2 us
    all_to_all x1, blocking collectives, body(): lax.all_to_all(tokens, 'dp', split_axis=1, concat_axis=0, tiled=True)  8.97 us
    all_gather x1, blocking collectives, body(): hidden_all = lax.all_gather(hidden_product, 'dp', axis=0, tiled=True)  8.74 us
    dot_general x1, matrix products, body(): jnp.dot(hidden_all, down_projection_matrix, preferred_element_type=jnp.fl...  7.51 us
    all_to_all x1, blocking collectives, body(): lax.all_to_all(rows_out.astype(jnp.bfloat16), 'dp', split_axis=0, concat_...  7.14 us
  transfers between devices with their start and end apart: 4, of which 4 were waited for; matrix products, arithmetic and copies ran while one was open for 11% of the time, Pallas kernels for 0%

commit v1 on v0

--- a/solution.py
+++ b/solution.py
@@ -20,7 +20,17 @@
 ):
     adapter_rank_size = gate_adapter_inmap.shape[1]
     columns = lax.all_to_all(tokens, "dp", split_axis=1, concat_axis=0, tiled=True)
-    gathered = lax.all_gather(columns, "tensor", axis=0, tiled=True)
+    array = columns
+    ways, here, step = (lax.axis_size("tensor"), lax.axis_index("tensor"), array.shape[0])
+    shape = [n * ways if d == 0 else n for d, n in enumerate(array.shape)]
+    gathered = lax.dynamic_update_slice_in_dim(
+        jnp.zeros(shape, array.dtype), array, here * step, axis=0
+    )
+    for far in range(1, ways):
+        array = lax.ppermute(array, "tensor", [(d, (d + 1) % ways) for d in range(ways)])
+        gathered = lax.dynamic_update_slice_in_dim(
+            gathered, array, (here - far) % ways * step, axis=0
+        )
 
     def summed(weights):
         partial = jnp.dot(gathered, weights, preferred_element_type=jnp.float32)

time: 182 us -> 183 us (level)
  blocking collectives: 41 us -> 15.9 us
  waiting for transfers between devices: 93.8 us -> 114 us
  starting transfers between devices: 0.13 us -> 6.61 us
  other arithmetic: 0.96 us -> 3.02 us
    ppermute x0 -> x3, waiting for transfers between devices: none -> 18.6 us  [body(): lax.ppermute(array, 'tensor', [(d, (d + 1) % ways) for d in range(ways)])]
    all_gather x1 -> x0, blocking collectives: 16.2 us -> none  [body(): gathered = lax.all_gather(columns, 'tensor', axis=0, tiled=True)]
    all_to_all x1 -> x0, blocking collectives: 8.97 us -> none  [body(): lax.all_to_all(tokens, 'dp', split_axis=1, concat_axis=0, tiled=True)]
    all_to_all x0 -> x1, waiting for transfers between devices: none -> 4.6 us  [body(): lax.all_to_all(tokens, 'dp', split_axis=1, concat_axis=0, tiled=True)]
    all_to_all x0 -> x1, starting transfers between devices: none -> 4.37 us  [body(): lax.all_to_all(tokens, 'dp', split_axis=1, concat_axis=0, tiled=True)]
    unnamed x5 -> x4, waiting for transfers between devices: 3.5 us -> 0.07 us
    ppermute x0 -> x3, starting transfers between devices: none -> 2.12 us  [body(): lax.ppermute(array, 'tensor', [(d, (d + 1) % ways) for d in range(ways)])]
    convert_element_type x0 -> x2, other arithmetic: none -> 2.05 us  [the longest x1 1.3 us: body(): (jax.nn.silu(gate_activated) * up_projected_value).astype(jnp.bfloat16)]
  transfers between devices with their start and end apart: 4 -> 8, of which waited for: 4 -> 7; matrix products, arithmetic and copies ran while one was open for 11% -> 10% of each run, Pallas kernels for 0% -> 0%
where the time goes in v1:
time: 183 us
  waiting for transfers between devices  114 us (62%)
  matrix products  29 us (16%)
  blocking collectives  15.9 us (9%)
  between operations  13.2 us (7%)
  starting transfers between devices  6.61 us (4%)
  other arithmetic  3.02 us (2%)
    reduce_scatter x3, waiting for transfers between devices, summed(): return lax.psum_scatter(partial, 'dp', scatter_dimension=0, tiled=True)  63 us
    reduce_scatter x1, waiting for transfers between devices, body(): rows_out = lax.psum_scatter(term, 'tensor', scatter_dimension=0, tiled=True)  28 us
    dot_general x3, matrix products, summed(): partial = jnp.dot(gathered, weights, preferred_element_type=jnp.float32)  19.1 us
    ppermute x3, waiting for transfers between devices, body(): lax.ppermute(array, 'tensor', [(d, (d + 1) % ways) for d in range(ways)])  18.6 us
    all_gather x1, blocking collectives, body(): hidden_all = lax.all_gather(hidden_product, 'dp', axis=0, tiled=True)  8.74 us
    dot_general x1, matrix products, body(): jnp.dot(hidden_all, down_projection_matrix, preferred_element_type=jnp.fl...  7.51 us
    all_to_all x1, blocking collectives, body(): lax.all_to_all(rows_out.astype(jnp.bfloat16), 'dp', split_axis=0, concat_...  7.14 us
    all_to_all x1, waiting for transfers between devices, body(): lax.all_to_all(tokens, 'dp', split_axis=1, concat_axis=0, tiled=True)  4.6 us
  transfers between devices with their start and end apart: 8, of which 7 were waited for; matrix products, arithmetic and copies ran while one was open for 10% of the time, Pallas kernels for 0%

profile of v1, /device:TPU:0, one launch (start us, length us, event | category | flops | bytes accessed | tf_op | source)
XLA Modules:
  0.0 182.7 jit_solution(447606287409007583)
XLA Ops:
  6.5 0.0 copy-start
  6.5 4.4 %all-to-all-start = ((bf16[8,4,2048]{2,0,1:T(8,128)(2,1)}), bf16[8,4,2048]{2,0,1:T(8,128)(2,1)S(1)}, u32[]{:S(2)}, u32[]{:S(2)}) async-start(bf16[8,4,2048]{2,0,1:T(8,128)(2,1)} %bitcast.24), calls=%async_computation | async-start | bytes 262144 | tf_op jit(solution)/shard_map/all_to_all | solution.py:22
  10.9 0.0 reduce-scatter.7.cloned.1.call-start
  10.9 4.6 %all-to-all-done = bf16[8,4,2048]{2,0,1:T(8,128)(2,1)S(1)} async-done(((bf16[8,4,2048]{2,0,1:T(8,128)(2,1)}), bf16[8,4,2048]{2,0,1:T(8,128)(2,1)S(1)}, u32[]{:S(2)}, u32[]{:S(2)}) %all-to-all-start) | async-done | bytes 131104 | tf_op jit(solution)/shard_map/all_to_all | solution.py:22
  15.5 2.1 %collective-permute-start = (bf16[32,2048]{1,0:T(8,128)(2,1)S(1)}, bf16[32,2048]{1,0:T(8,128)(2,1)S(1)}, u32[]{:S(2)}, u32[]{:S(2)}) collective-permute-start(bf16[32,2048]{1,0:T(8,128)(2,1)S(1)} %bitcast.22), channel_id=1, source_target_pairs={{0,4},{4,8},{8,12},{12,0},{1,5},{5,9},{9,13},{13,1},{2,6},{6,10},{... | collective-permute-start | bytes 393224 | tf_op jit(solution)/shard_map/ppermute | solution.py:30
  17.7 5.1 %collective-permute-done = bf16[32,2048]{1,0:T(8,128)(2,1)S(1)} collective-permute-done((bf16[32,2048]{1,0:T(8,128)(2,1)S(1)}, bf16[32,2048]{1,0:T(8,128)(2,1)S(1)}, u32[]{:S(2)}, u32[]{:S(2)}) %collective-permute-start) | collective-permute-done | bytes 131104 | tf_op jit(solution)/shard_map/ppermute | solution.py:30
  22.8 0.0 collective-permute-start.1
  22.8 6.7 %collective-permute-done.1 = bf16[32,2048]{1,0:T(8,128)(2,1)S(1)} collective-permute-done((bf16[32,2048]{1,0:T(8,128)(2,1)S(1)}, bf16[32,2048]{1,0:T(8,128)(2,1)S(1)}, u32[]{:S(2)}, u32[]{:S(2)}) %collective-permute-start.1) | collective-permute-done | bytes 131104 | tf_op jit(solution)/shard_map/ppermute | solution.py:30
  29.5 0.0 collective-permute-start.2
  29.6 6.7 %collective-permute-done.2 = bf16[32,2048]{1,0:T(8,128)(2,1)S(1)} collective-permute-done((bf16[32,2048]{1,0:T(8,128)(2,1)S(1)}, bf16[32,2048]{1,0:T(8,128)(2,1)S(1)}, u32[]{:S(2)}, u32[]{:S(2)}) %collective-permute-start.2) | collective-permute-done | bytes 131104 | tf_op jit(solution)/shard_map/ppermute | solution.py:30
  36.3 2.0 %fusion.1 = f32[128,128]{1,0:T(8,128)} fusion(bf16[128,2048]{1,0:T(8,128)(2,1)S(1)} %constant_dynamic-update-slice_fusion, bf16[2048,64]{0,1:T(8,128)(2,1)} %param.16, bf16[2048,64]{0,1:T(8,128)(2,1)} %param.14), kind=kOutput, calls=%fused_computation.4 | convolution fusion | flops 68157440 | bytes 1114112 | tf_op jit(solution)/shard_map/dot_general | solution.py:36
  38.3 0.0 reduce-scatter.7.cloned.1.call-update
  38.3 0.0 reduce-scatter.5.cloned.1.call-start
  38.4 8.6 %fusion.10 = f32[128,3584]{1,0:T(8,128)} fusion(bf16[128,2048]{1,0:T(8,128)(2,1)S(1)} %constant_dynamic-update-slice_fusion, bf16[2048,3584]{1,0:T(8,128)(2,1)} %param.11), kind=kOutput, calls=%fused_computation.19 | convolution fusion | flops 1879048192 | bytes 17039360 | tf_op jit(solution)/shard_map/dot_general | solution.py:36
  46.9 0.0 copy-start.1
  46.9 0.0 copy-start.2
  46.9 0.0 reduce-scatter.5.cloned.1.call-update
  46.9 0.0 reduce-scatter.9.cloned.1.call-start
  47.0 8.6 %fusion.11 = f32[128,3584]{1,0:T(8,128)} fusion(bf16[128,2048]{1,0:T(8,128)(2,1)S(1)} %constant_dynamic-update-slice_fusion, bf16[2048,3584]{1,0:T(8,128)(2,1)} %param.12), kind=kOutput, calls=%fused_computation.20 | convolution fusion | flops 1879048192 | bytes 17039360 | tf_op jit(solution)/shard_map/dot_general | solution.py:36
  55.6 0.0 copy-start.3
  55.6 0.0 reduce-scatter.9.cloned.1.call-update
  55.6 0.0 reduce-scatter.11.cloned.1.call-start
  55.6 0.0 reduce-scatter.7.cloned.1.call-done
  55.7 0.8 convert_element_type.10
  56.4 0.0 copy-done.1
  56.4 0.3 convolution_multiply_fusion
  56.7 0.0 copy-done.2
  56.7 0.2 convolution_multiply_fusion.1
  56.9 30.8 %reduce-scatter.5.cloned.1.call-done = f32[32,3584]{1,0:T(8,128)} async-done(((f32[128,3584]{1,0:T(8,128)}), f32[32,3584]{1,0:T(8,128)}) %reduce-scatter.5.cloned.1.call-update) | async-done | bytes 458768 | tf_op jit(solution)/shard_map/reduce_scatter | solution.py:37
  87.7 32.2 %reduce-scatter.9.cloned.1.call-done = f32[32,3584]{1,0:T(8,128)} async-done(((f32[128,3584]{1,0:T(8,128)}), f32[32,3584]{1,0:T(8,128)}) %reduce-scatter.9.cloned.1.call-update) | async-done | bytes 458768 | tf_op jit(solution)/shard_map/reduce_scatter | solution.py:37
  119.9 1.3 multiply_convert_fusion
  121.2 8.7 %all_gather.3 = bf16[128,3584]{1,0:T(8,128)(2,1)S(1)} all-gather(bf16[32,3584]{1,0:T(8,128)(2,1)S(1)} %multiply_convert_fusion), channel_id=1, replica_groups=mesh['groups'=2,'tensor'=4,'dp'=4] {'dp'}, dimensions={0}, use_global_device_ids=true | all-gather | bytes 1146880 | tf_op jit(solution)/shard_map/all_gather | solution.py:53
  129.9 7.5 %fusion.12 = f32[128,2048]{1,0:T(8,128)S(1)} fusion(bf16[128,3584]{1,0:T(8,128)(2,1)S(1)} %all_gather.3, bf16[3584,2048]{1,0:T(8,128)(2,1)} %param.13), kind=kOutput, calls=%fused_computation.21 | convolution fusion | flops 1879048192 | bytes 16646144 | tf_op jit(solution)/shard_map/dot_general | solution.py:59
  137.5 0.0 copy-done.3
  137.5 0.4 fusion.13
  137.9 0.0 copy-done
  137.9 1.6 fusion
  139.4 0.0 reduce-scatter.11.cloned.1.call-update
  139.5 28.0 %reduce-scatter.11.cloned.1.call-done = f32[32,2048]{1,0:T(8,128)} async-done(((f32[128,2048]{1,0:T(8,128)}), f32[32,2048]{1,0:T(8,128)}) %reduce-scatter.11.cloned.1.call-update) | async-done | bytes 262160 | tf_op jit(solution)/shard_map/reduce_scatter | solution.py:61
  167.4 1.0 convert_bitcast_fusion
  168.4 7.1 %all_to_all.38 = bf16[4,8,2048]{2,1,0:T(8,128)(2,1)S(1)} all-to-all(bf16[4,8,2048]{2,1,0:T(8,128)(2,1)S(1)} %convert_bitcast_fusion), channel_id=1, replica_groups=mesh['groups'=2,'tensor'=4,'dp'=4] {'dp'}, dimensions={0} | all-to-all | bytes 262144 | tf_op jit(solution)/shard_map/all_to_all | solution.py:62
  175.5 0.7 copy.16
  (5 shorter events, 0.1 us)
Async XLA Ops:
  6.5 131.3 %copy-start = (bf16[64,8192]{1,0:T(8,128)(2,1)S(1)}, bf16[64,8192]{1,0:T(8,128)(2,1)}, u32[]{:S(2)}) copy-start(bf16[64,8192]{1,0:T(8,128)(2,1)} %param.19) | copy-start | bytes 3145732
  6.5 9.0 %all-to-all-start = ((bf16[8,4,2048]{2,0,1:T(8,128)(2,1)}), bf16[8,4,2048]{2,0,1:T(8,128)(2,1)S(1)}, u32[]{:S(2)}, u32[]{:S(2)}) async-start(bf16[8,4,2048]{2,0,1:T(8,128)(2,1)} %bitcast.24), calls=%async_computation | async-start | bytes 262144 | tf_op jit(solution)/shard_map/all_to_all | solution.py:22
  10.9 44.8 %reduce-scatter.7.cloned.1.call-start = ((), (), s32[]{:S(2)}) async-start(), calls=%async_computation.7 | async-start | bytes 81920 | tf_op jit(solution)/shard_map/reduce_scatter | solution.py:37
  15.5 7.3 %collective-permute-start = (bf16[32,2048]{1,0:T(8,128)(2,1)S(1)}, bf16[32,2048]{1,0:T(8,128)(2,1)S(1)}, u32[]{:S(2)}, u32[]{:S(2)}) collective-permute-start(bf16[32,2048]{1,0:T(8,128)(2,1)S(1)} %bitcast.22), channel_id=1, source_target_pairs={{0,4},{4,8},{8,12},{12,0},{1,5},{5,9},{9,13},{13,1},{2,6},{6,10},{... | collective-permute-start | bytes 393224 | tf_op jit(solution)/shard_map/ppermute | solution.py:30
  22.8 6.8 %collective-permute-start.1 = (bf16[32,2048]{1,0:T(8,128)(2,1)S(1)}, bf16[32,2048]{1,0:T(8,128)(2,1)S(1)}, u32[]{:S(2)}, u32[]{:S(2)}) collective-permute-start(bf16[32,2048]{1,0:T(8,128)(2,1)S(1)} %collective-permute-done), channel_id=1, source_target_pairs={{0,4},{4,8},{8,12},{12,0},{1,5},{5,9},{9,13},{13,1},{2,6},{6,10},{... | collective-permute-start | bytes 393224 | tf_op jit(solution)/shard_map/ppermute | solution.py:30
  29.5 6.8 %collective-permute-start.2 = (bf16[32,2048]{1,0:T(8,128)(2,1)S(1)}, bf16[32,2048]{1,0:T(8,128)(2,1)S(1)}, u32[]{:S(2)}, u32[]{:S(2)}) collective-permute-start(bf16[32,2048]{1,0:T(8,128)(2,1)S(1)} %collective-permute-done.1), channel_id=1, source_target_pairs={{0,4},{4,8},{8,12},{12,0},{1,5},{5,9},{9,13},{13,1},{2,6},{6,10},{... | collective-permute-start | bytes 393224 | tf_op jit(solution)/shard_map/ppermute | solution.py:30
  38.3 49.4 %reduce-scatter.5.cloned.1.call-start = ((), (), s32[]{:S(2)}) async-start(), calls=%async_computation.6 | async-start | bytes 2293760 | tf_op jit(solution)/shard_map/reduce_scatter | solution.py:37
  46.9 9.5 %copy-start.1 = (bf16[64,3584]{1,0:T(8,128)(2,1)S(1)}, bf16[64,3584]{1,0:T(8,128)(2,1)}, u32[]{:S(2)}) copy-start(bf16[64,3584]{1,0:T(8,128)(2,1)} %param.17) | copy-start | bytes 1376260
  46.9 9.8 %copy-start.2 = (bf16[64,3584]{1,0:T(8,128)(2,1)S(1)}, bf16[64,3584]{1,0:T(8,128)(2,1)}, u32[]{:S(2)}) copy-start(bf16[64,3584]{1,0:T(8,128)(2,1)} %param.15) | copy-start | bytes 1376260
  46.9 73.0 %reduce-scatter.9.cloned.1.call-start = ((), (), s32[]{:S(2)}) async-start(), calls=%async_computation.8 | async-start | bytes 2293760 | tf_op jit(solution)/shard_map/reduce_scatter | solution.py:37
  55.6 81.9 %copy-start.3 = (bf16[3584,64]{0,1:T(8,128)(2,1)S(1)}, bf16[3584,64]{0,1:T(8,128)(2,1)}, u32[]{:S(2)}) copy-start(bf16[3584,64]{0,1:T(8,128)(2,1)} %param.18) | copy-start | bytes 1376260
  55.6 111.8 %reduce-scatter.11.cloned.1.call-start = ((), (), s32[]{:S(2)}) async-start(), calls=%async_computation.9 | async-start | bytes 1310720 | tf_op jit(solution)/shard_map/reduce_scatter | solution.py:61
Sparse Core Ops, SparseCore 0:
  38.4 17.1 reduce-scatter.6
  58.1 29.5 reduce-scatter.4
  90.3 29.5 reduce-scatter.8
  139.6 27.8 reduce-scatter.10
